TPU v7x, 32 devices: a whole 2x2x4 slice. The times are simulated.
32 devices in a mesh: elem: 8 (over z, core), front: 4 (over y, x).
Axes of the slice: x: 2, y: 2, z: 4, core: 2. Of those that a mesh axis runs over, the one named last changes fastest.
Arguments:
- elem_mat: bfloat16 [24, 24, 4096], P(None, None, ('elem', 'front')), may hold values from -1.25 to 1.25
- elem_deriv: bfloat16 [24, 24, 4096], P(None, None, ('elem', 'front')), may hold values from -1.1953125 to 1.1953125
- elem_disp: bfloat16 [24, 4096], P(None, ('elem', 'front')), may hold values from -6 to 6
- elem_sens: bfloat16 [4096, 24, 512], P(('elem', 'front')), may hold values from -3 to 3
- design_var: int32 [4096], P(('elem', 'front')), may hold values from 0 to 511
- dof_rows: int32 [24, 4096], P(None, ('elem', 'front')), may hold values from 0 to 14336, as said below
- inverse_factor: bfloat16 [57344, 8192], P('front', 'elem'), may hold values from -2 to 2
- coupling: bfloat16 [8192, 49152], P('elem', 'front'), may hold values from -0.0625 to 0.0625
- front_sizes: int32 [7], replicated, may hold values from 4096 to 8192
Outputs:
- sens: float32 [57344, 512], P('front', 'elem')
Inputs may be any that keep to these rules, and one draw needn't show every extreme that they name: `dof_rows`: the used rows of one element lie in one aligned block of 128 rows; the value 14336 marks a degree of freedom that no front holds.
All inputs are finite; a program needn't handle non-finite values.
Results may differ from a plain program's by a relative error of at most 0.014.
Values may be sent and summed in bfloat16 or wider, within the bound.
A program may use at most 128 MiB of HBM per device.

v0:
```python
import jax
import jax.numpy as jnp
from jax import lax
from jax.sharding import PartitionSpec as P

FS = 8192
LEVELS = 3


def swapped(array, axis, bit):
    return lax.ppermute(array, axis, [(i, i ^ 1 << bit) for i in range(lax.axis_size(axis))])


def form_loads(tables, derivs, disps, sens_block, variables, places, column_base, spot_rows):
    column_count = sens_block.shape[2]
    pseudo = -jnp.einsum("ije,ejc->eic", tables, sens_block, preferred_element_type=jnp.float32)
    drive_term = -jnp.einsum("ije,je->ei", derivs, disps, preferred_element_type=jnp.float32)
    column_ids = column_base + lax.iota(jnp.int32, column_count)
    hit_column = (column_ids[None, :] == variables[:, None]).astype(jnp.float32)
    pseudo = pseudo + drive_term[:, :, None] * hit_column[:, None, :]
    term_rows = jnp.zeros((spot_rows, column_count), jnp.float32)
    return term_rows.at[places.T.reshape(-1)].add(pseudo.reshape(-1, column_count), mode="drop")


def gather_group(local_block, bit_count, device):
    if bit_count == 0:
        return local_block
    for bit_at in range(bit_count):
        partner = swapped(local_block, "front", bit_at)
        is_upper = device >> bit_at & 1 == 1
        local_block = jnp.where(
            is_upper,
            jnp.concatenate([partner, local_block], 0),
            jnp.concatenate([local_block, partner], 0),
        )
    return local_block


def reduce_group(partial_value, bit_count, device):
    if bit_count == 0:
        return partial_value
    for bit_at in reversed(range(bit_count)):
        half_rows = partial_value.shape[0] // 2
        lower_half = partial_value[:half_rows]
        upper_half = partial_value[half_rows:]
        is_upper = device >> bit_at & 1 == 1
        kept_half = jnp.where(is_upper, upper_half, lower_half)
        sent_half = jnp.where(is_upper, lower_half, upper_half)
        partial_value = kept_half + swapped(sent_half, "front", bit_at)
    return partial_value


def to_row_block(local_block, bit_count, device):
    whole_front = gather_group(local_block, bit_count, device)
    return lax.all_to_all(whole_front, "elem", split_axis=0, concat_axis=1, tiled=True)


def from_row_block(partial_value, bit_count, device):
    spread = lax.all_to_all(partial_value, "elem", split_axis=1, concat_axis=0, tiled=True)
    return reduce_group(spread, bit_count, device)


def body(
    elem_mat,
    elem_deriv,
    elem_disp,
    elem_sens,
    design_var,
    dof_rows,
    inverse_factor,
    coupling,
    front_sizes,
):
    front_count = lax.axis_size("front")
    depth_bits = front_count.bit_length() - 1
    device = lax.axis_index("front")
    spot_rows = inverse_factor.shape[0]
    own_sens = lax.all_to_all(elem_sens, "elem", split_axis=2, concat_axis=0, tiled=True)
    tables, derivs, disps = (
        lax.all_gather(elem_mat, "elem", axis=2, tiled=True),
        lax.all_gather(elem_deriv, "elem", axis=2, tiled=True),
        lax.all_gather(elem_disp, "elem", axis=1, tiled=True),
    )
    variables, places = (
        lax.all_gather(design_var, "elem", axis=0, tiled=True),
        lax.all_gather(dof_rows, "elem", axis=1, tiled=True),
    )
    column_base = lax.axis_index("elem") * own_sens.shape[2]
    load_rows = form_loads(
        tables, derivs, disps, own_sens, variables, places, column_base, spot_rows
    )
    level_facts = []
    offset = 0
    first_front = 0
    for level_at in range(LEVELS):
        bit_count = depth_bits - (LEVELS - 1 - level_at)
        block_rows = FS >> bit_count
        front_id = first_front + (device >> bit_count)
        size_now = lax.dynamic_index_in_dim(front_sizes, front_id, 0, keepdims=False)
        rows_at = (device & (1 << bit_count) - 1) * block_rows + lax.iota(jnp.int32, block_rows)
        live_rows = (rows_at < size_now).astype(jnp.float32)[:, None]
        level_facts.append((bit_count, block_rows, offset, live_rows))
        offset = offset + block_rows
        first_front = first_front + (1 << LEVELS - 1 - level_at)
    forward_out = []
    acc_rows = None
    for level_at in range(LEVELS):
        bit_count, block_rows, offset, live_rows = level_facts[level_at]
        given = load_rows[offset : offset + block_rows]
        if acc_rows is not None:
            given = given - acc_rows
        rhs_in = (live_rows * given).astype(jnp.bfloat16)
        rhs_rows = to_row_block(rhs_in, bit_count, device)
        factor_rows = inverse_factor[offset : offset + block_rows]
        partial_value = jnp.dot(factor_rows, rhs_rows, preferred_element_type=jnp.float32)
        solved = live_rows * lax.psum_scatter(
            partial_value, "elem", scatter_dimension=1, tiled=True
        )
        forward_out.append(solved)
        if level_at < LEVELS - 1:
            wide_solved = lax.all_gather(solved.astype(jnp.bfloat16), "elem", axis=1, tiled=True)
            links = coupling[:, offset : offset + block_rows]
            parent_part = jnp.dot(links, wide_solved, preferred_element_type=jnp.float32)
            acc_rows = from_row_block(parent_part, bit_count + 1, device)
    pieces_out = [None] * LEVELS
    parent_rows = None
    for level_at in reversed(range(LEVELS)):
        bit_count, block_rows, offset, live_rows = level_facts[level_at]
        residual = forward_out[level_at]
        if parent_rows is not None:
            parent_block = to_row_block(parent_rows, bit_count + 1, device)
            links = coupling[:, offset : offset + block_rows]
            correction = lax.dot_general(
                links, parent_block, (((0,), (0,)), ((), ())), preferred_element_type=jnp.float32
            )
            residual = residual - lax.psum_scatter(
                correction, "elem", scatter_dimension=1, tiled=True
            )
        back_in = (live_rows * residual).astype(jnp.bfloat16)
        wide_back = lax.all_gather(back_in, "elem", axis=1, tiled=True)
        factor_rows = inverse_factor[offset : offset + block_rows]
        partial_value = lax.dot_general(
            factor_rows, wide_back, (((0,), (0,)), ((), ())), preferred_element_type=jnp.float32
        )
        answer = live_rows * from_row_block(partial_value, bit_count, device)
        pieces_out[level_at] = answer
        parent_rows = answer.astype(jnp.bfloat16)
    return jnp.concatenate(pieces_out, 0)


def solution(mesh):
    return jax.shard_map(
        body,
        mesh=mesh,
        in_specs=(
            P(None, None, ("elem", "front")),
            P(None, None, ("elem", "front")),
            P(None, ("elem", "front")),
            P(("elem", "front"), None, None),
            P(("elem", "front")),
            P(None, ("elem", "front")),
            P("front", "elem"),
            P("elem", "front"),
            P(),
        ),
        out_specs=P("front", "elem"),
        check_vma=False,
    )
```

profile of v0, /device:TPU:0, one launch (start us, length us, event | category | flops | bytes accessed | tf_op | source)
XLA Modules:
  0.0 1891.1 jit_solution(9125538343845212889)
XLA Ops:
  7.3 5.3 copy.36
  12.6 6.5 all-to-all-start
  19.9 95.3 %all_gather.30 = s32[24,1024]{1,0:T(8,128)S(1)} all-gather(s32[24,128]{1,0:T(8,128)S(1)} %copy-done.3), channel_id=1, replica_groups=mesh['elem'=8,'front'=4] {'elem'}, dimensions={1}, use_global_device_ids=true | all-gather | bytes 110592 | tf_op jit(solution)/shard_map/all_gather | solution.py:86
  118.3 11.1 all-gather
  129.5 12.7 all_gather.33
  143.8 1.7 multiply_reduce_fusion
  146.4 1.9 neg.7
  148.3 7.5 copy.39
  155.8 5.9 copy.38
  161.7 9.3 multiply_add_fusion
  171.0 134.3 %scatter_custom_fusion = f32[14336,64]{1,0:T(8,128)} fusion(s32[24576]{0:T(1024)S(1)} %bitcast.156, f32[24576,64]{1,0:T(8,128)} %bitcast.120, f32[]{:T(128)} %constant.14.clone.1), kind=kCustom, calls=%fused_computation.27 | custom fusion | flops 1572864 | bytes 3670528 | tf_op jit(solution)/shard_map/scatter-add | solution.py:22
  305.2 4.4 slice.93
  309.7 2.8 copy.65
  312.7 29.4 %all_to_all.184 = bf16[8,1024,64]{1,2,0:T(8,128)(2,1)S(1)} all-to-all(bf16[8,1024,64]{1,2,0:T(8,128)(2,1)S(1)} %bitcast.137), channel_id=1, replica_groups=mesh['elem'=8,'front'=4] {'elem'}, dimensions={0} | all-to-all | bytes 2097152 | tf_op jit(solution)/shard_map/all_to_all | solution.py:55
  342.2 15.8 fusion.8
  358.1 167.1 %reduce-scatter.6.cloned.1.call-done = f32[8192,64]{0,1:T(8,128)} async-done(((f32[8192,512]{0,1:T(8,128)}), f32[8192,64]{0,1:T(8,128)}) %reduce-scatter.6.cloned.1.call-update) | async-done | bytes 2097168 | tf_op jit(solution)/shard_map/reduce_scatter | solution.py:116
  525.2 2.7 multiply_convert_fusion.2
  527.9 80.7 %all-gather.13.cloned.1.call-done = bf16[8192,512]{0,1:T(8,128)(2,1)} async-done(((bf16[8192,64]{0,1:T(8,128)(2,1)}), bf16[8192,512]{0,1:T(8,128)(2,1)}) %all-gather.13.cloned.1.call-update) | async-done | bytes 8388624 | tf_op jit(solution)/shard_map/all_gather | solution.py:121
  608.6 15.8 fusion.2
  624.4 3.6 all-to-all-start.2
  628.1 48.9 %all-to-all-done.2 = f32[1024,8,64]{0,2,1:T(8,128)S(1)} async-done(((f32[1024,8,64]{0,2,1:T(8,128)}), f32[1024,8,64]{0,2,1:T(8,128)S(1)}, u32[]{:S(2)}, u32[]{:S(2)}) %all-to-all-start.2) | async-done | bytes 2097184 | tf_op jit(solution)/shard_map/all_to_all | solution.py:59
  683.2 21.0 %collective-permute-done = f32[4096,64]{0,1:T(8,128)} collective-permute-done((f32[4096,64]{0,1:T(8,128)}, f32[4096,64]{0,1:T(8,128)}, u32[]{:S(2)}, u32[]{:S(2)}) %collective-permute-start) | collective-permute-done | bytes 1048608 | tf_op jit(solution)/shard_map/ppermute | solution.py:11
  707.1 11.0 collective-permute-done.1
  718.5 29.9 %all_to_all.185 = bf16[8,1024,64]{1,2,0:T(8,128)(2,1)S(1)} all-to-all(bf16[8,1024,64]{1,2,0:T(8,128)(2,1)S(1)} %bitcast.138), channel_id=1, replica_groups=mesh['elem'=8,'front'=4] {'elem'}, dimensions={0} | all-to-all | bytes 2097152 | tf_op jit(solution)/shard_map/all_to_all | solution.py:55
  748.4 10.1 fusion.22
  758.8 88.3 %reduce-scatter.8.cloned.1.call-done = f32[4096,64]{0,1:T(8,128)} async-done(((f32[4096,512]{0,1:T(8,128)}), f32[4096,64]{0,1:T(8,128)}) %reduce-scatter.8.cloned.1.call-update) | async-done | bytes 1048592 | tf_op jit(solution)/shard_map/reduce_scatter | solution.py:116
  847.2 2.1 multiply_convert_fusion.5
  849.3 45.5 %all-gather.15.cloned.1.call-done = bf16[4096,512]{0,1:T(8,128)(2,1)} async-done(((bf16[4096,64]{0,1:T(8,128)(2,1)}), bf16[4096,512]{0,1:T(8,128)(2,1)}) %all-gather.15.cloned.1.call-update) | async-done | bytes 4194320 | tf_op jit(solution)/shard_map/all_gather | solution.py:121
  894.7 10.5 fusion.16
  905.2 3.6 all-to-all-start.4
  908.9 48.9 %all-to-all-done.4 = f32[1024,8,64]{0,2,1:T(8,128)S(1)} async-done(((f32[1024,8,64]{0,2,1:T(8,128)}), f32[1024,8,64]{0,2,1:T(8,128)S(1)}, u32[]{:S(2)}, u32[]{:S(2)}) %all-to-all-start.4) | async-done | bytes 2097184 | tf_op jit(solution)/shard_map/all_to_all | solution.py:59
  958.2 1.5 collective-permute-start.2
  959.8 23.0 %collective-permute-done.2 = f32[4096,64]{0,1:T(8,128)S(1)} collective-permute-done((f32[4096,64]{0,1:T(8,128)S(1)}, f32[4096,64]{0,1:T(8,128)S(1)}, u32[]{:S(2)}, u32[]{:S(2)}) %collective-permute-start.2) | collective-permute-done | bytes 1048608 | tf_op jit(solution)/shard_map/ppermute | solution.py:11
  985.5 10.2 collective-permute-done.3
  998.4 4.9 collective-permute-done.4
  1005.0 9.0 collective-permute-done.5
  1014.3 30.9 %all_to_all.186 = bf16[8,1024,64]{1,2,0:T(8,128)(2,1)S(1)} all-to-all(bf16[8,1024,64]{1,2,0:T(8,128)(2,1)S(1)} %bitcast.139), channel_id=1, replica_groups=mesh['elem'=8,'front'=4] {'elem'}, dimensions={0} | all-to-all | bytes 2097152 | tf_op jit(solution)/shard_map/all_to_all | solution.py:55
  1045.3 6.5 fusion.34
  1051.9 48.9 %reduce-scatter.10.cloned.1.call-done = f32[2048,64]{0,1:T(8,128)} async-done(((f32[2048,512]{0,1:T(8,128)}), f32[2048,64]{0,1:T(8,128)}) %reduce-scatter.10.cloned.1.call-update) | async-done | bytes 524304 | tf_op jit(solution)/shard_map/reduce_scatter | solution.py:116
  1100.8 1.8 multiply_convert_fusion.6
  1102.6 27.7 %all-gather.17.cloned.1.call-done = bf16[2048,512]{0,1:T(8,128)(2,1)} async-done(((bf16[2048,64]{0,1:T(8,128)(2,1)}), bf16[2048,512]{0,1:T(8,128)(2,1)}) %all-gather.17.cloned.1.call-update) | async-done | bytes 2097168 | tf_op jit(solution)/shard_map/all_gather | solution.py:140
  1130.4 5.1 fusion.28
  1135.5 51.9 %all_to_all.187 = f32[1024,8,64]{0,2,1:T(8,128)S(1)} all-to-all(f32[1024,8,64]{0,2,1:T(8,128)S(1)} %bitcast.144), channel_id=1, replica_groups=mesh['elem'=8,'front'=4] {'elem'}, dimensions={1} | all-to-all | bytes 4194304 | tf_op jit(solution)/shard_map/all_to_all | solution.py:59
  1189.5 23.0 %collective-permute-done.6 = f32[4096,64]{0,1:T(8,128)S(1)} collective-permute-done((f32[4096,64]{0,1:T(8,128)S(1)}, f32[4096,64]{0,1:T(8,128)S(1)}, u32[]{:S(2)}, u32[]{:S(2)}) %collective-permute-start.6) | collective-permute-done | bytes 1048608 | tf_op jit(solution)/shard_map/ppermute | solution.py:11
  1214.2 11.0 collective-permute-done.7
  1227.5 4.9 collective-permute-done.8
  1234.1 9.0 collective-permute-done.9
  1243.3 31.4 %all_to_all.188 = bf16[8,1024,64]{1,2,0:T(8,128)(2,1)S(1)} all-to-all(bf16[8,1024,64]{1,2,0:T(8,128)(2,1)S(1)} %bitcast.140), channel_id=1, replica_groups=mesh['elem'=8,'front'=4] {'elem'}, dimensions={0} | all-to-all | bytes 2097152 | tf_op jit(solution)/shard_map/all_to_all | solution.py:55
  1274.7 10.1 fusion.25
  1284.9 88.5 %reduce-scatter.12.cloned.1.call-done = f32[4096,64]{0,1:T(8,128)} async-done(((f32[4096,512]{0,1:T(8,128)}), f32[4096,64]{0,1:T(8,128)}) %reduce-scatter.12.cloned.1.call-update) | async-done | bytes 1048592 | tf_op jit(solution)/shard_map/reduce_scatter | solution.py:136
  1373.4 2.1 multiply_convert_fusion.3
  1375.6 45.4 %all-gather.19.cloned.1.call-done = bf16[4096,512]{0,1:T(8,128)(2,1)} async-done(((bf16[4096,64]{0,1:T(8,128)(2,1)}), bf16[4096,512]{0,1:T(8,128)(2,1)}) %all-gather.19.cloned.1.call-update) | async-done | bytes 4194320 | tf_op jit(solution)/shard_map/all_gather | solution.py:140
  1421.1 8.1 fusion.18
  1429.2 51.5 %all_to_all.189 = f32[1024,8,64]{0,2,1:T(8,128)S(1)} all-to-all(f32[1024,8,64]{0,2,1:T(8,128)S(1)} %bitcast.145), channel_id=1, replica_groups=mesh['elem'=8,'front'=4] {'elem'}, dimensions={1} | all-to-all | bytes 4194304 | tf_op jit(solution)/shard_map/all_to_all | solution.py:59
  1482.7 23.0 %collective-permute-done.10 = f32[4096,64]{0,1:T(8,128)S(1)} collective-permute-done((f32[4096,64]{0,1:T(8,128)S(1)}, f32[4096,64]{0,1:T(8,128)S(1)}, u32[]{:S(2)}, u32[]{:S(2)}) %collective-permute-start.10) | collective-permute-done | bytes 1048608 | tf_op jit(solution)/shard_map/ppermute | solution.py:11
  1507.4 11.0 collective-permute-done.11
  1518.7 30.1 %all_to_all.190 = bf16[8,1024,64]{1,2,0:T(8,128)(2,1)S(1)} all-to-all(bf16[8,1024,64]{1,2,0:T(8,128)(2,1)S(1)} %bitcast.141), channel_id=1, replica_groups=mesh['elem'=8,'front'=4] {'elem'}, dimensions={0} | all-to-all | bytes 2097152 | tf_op jit(solution)/shard_map/all_to_all | solution.py:55
  1548.8 15.7 fusion.11
  1564.6 167.1 %reduce-scatter.14.cloned.1.call-done = f32[8192,64]{0,1:T(8,128)} async-done(((f32[8192,512]{0,1:T(8,128)}), f32[8192,64]{0,1:T(8,128)}) %reduce-scatter.14.cloned.1.call-update) | async-done | bytes 2097168 | tf_op jit(solution)/shard_map/reduce_scatter | solution.py:136
  1731.7 2.8 multiply_convert_fusion
  1734.5 80.6 %all-gather.21.cloned.1.call-done = bf16[8192,512]{0,1:T(8,128)(2,1)} async-done(((bf16[8192,64]{0,1:T(8,128)(2,1)}), bf16[8192,512]{0,1:T(8,128)(2,1)}) %all-gather.21.cloned.1.call-update) | async-done | bytes 8388624 | tf_op jit(solution)/shard_map/all_gather | solution.py:140
  1815.2 14.3 fusion.4
  1829.4 51.5 %all_to_all.191 = f32[1024,8,64]{0,2,1:T(8,128)S(1)} all-to-all(f32[1024,8,64]{0,2,1:T(8,128)S(1)} %bitcast.146), channel_id=1, replica_groups=mesh['elem'=8,'front'=4] {'elem'}, dimensions={1} | all-to-all | bytes 4194304 | tf_op jit(solution)/shard_map/all_to_all | solution.py:59
  1882.0 2.1 pad_maximum_fusion
  (103 shorter events, 38.3 us)
Async XLA Ops:
  6.5 137.2 %all-gather.11.cloned.1.call-start = ((), (), s32[]{:S(2)}) async-start(), calls=%async_computation.17 | async-start | bytes 1327104 | tf_op jit(solution)/shard_map/all_gather | solution.py:81
  12.6 7.3 copy-start.3
  12.6 105.1 %copy-start.5 = (s32[7]{0:T(128)S(1)}, s32[7]{0:T(128)}, u32[]{:S(2)}) copy-start(s32[7]{0:T(128)} %param.17) | copy-start | bytes 88
  12.6 105.7 %copy-start.6 = (s32[128]{0:T(128)S(1)}, s32[128]{0:T(128)}, u32[]{:S(2)}) copy-start(s32[128]{0:T(128)} %param.13) | copy-start | bytes 1540
  12.6 116.9 %copy-start.4 = (bf16[24,128]{1,0:T(8,128)(2,1)S(1)}, bf16[24,128]{1,0:T(8,128)(2,1)}, u32[]{:S(2)}) copy-start(bf16[24,128]{1,0:T(8,128)(2,1)} %param.11) | copy-start | bytes 18436
  12.6 143.2 %all-to-all-start = ((bf16[128,24,512]{0,1,2:T(8,128)(2,1)}), bf16[128,24,512]{0,1,2:T(8,128)(2,1)S(1)}, u32[]{:S(2)}, u32[]{:S(2)}) async-start(bf16[128,24,512]{0,1,2:T(8,128)(2,1)} %copy.36), calls=%async_computation | async-start | bytes 6291456 | tf_op jit(solution)/shard_map/all_to_all | solution.py:78
  19.1 129.2 %all-gather.9.cloned.1.call-start = ((), (), s32[]{:S(2)}) async-start(), calls=%async_computation.16 | async-start | bytes 1327104 | tf_op jit(solution)/shard_map/all_gather | solution.py:80
  19.9 505.4 %reduce-scatter.6.cloned.1.call-start = ((), (), s32[]{:S(2)}) async-start(), calls=%async_computation.18 | async-start | bytes 18874368 | tf_op jit(solution)/shard_map/reduce_scatter | solution.py:116
  358.1 250.5 %all-gather.13.cloned.1.call-start = ((), (), s32[]{:S(2)}) async-start(), calls=%async_computation.19 | async-start | bytes 9437184 | tf_op jit(solution)/shard_map/all_gather | solution.py:121
  624.4 52.6 %all-to-all-start.2 = ((f32[1024,8,64]{0,2,1:T(8,128)}), f32[1024,8,64]{0,2,1:T(8,128)S(1)}, u32[]{:S(2)}, u32[]{:S(2)}) async-start(f32[1024,8,64]{0,2,1:T(8,128)} %bitcast.143), calls=%async_computation.3 | async-start | bytes 4194304 | tf_op jit(solution)/shard_map/all_to_all | solution.py:59
  628.0 219.1 %reduce-scatter.8.cloned.1.call-start = ((), (), s32[]{:S(2)}) async-start(), calls=%async_computation.20 | async-start | bytes 9437184 | tf_op jit(solution)/shard_map/reduce_scatter | solution.py:116
  678.2 3.1 slice-start
  679.2 24.9 %collective-permute-start = (f32[4096,64]{0,1:T(8,128)}, f32[4096,64]{0,1:T(8,128)}, u32[]{:S(2)}, u32[]{:S(2)}) collective-permute-start(f32[4096,64]{0,1:T(8,128)} %bitcast.67), channel_id=1, source_target_pairs={{0,1},{1,0},{2,3},{3,2},{4,5},{5,4},{6,7},{7,6},{8,9},{9,8},{10,11... | collective-permute-start | bytes 3145736 | tf_op jit(solution)/shard_map/ppermute | solution.py:11
  705.6 12.6 collective-permute-start.1
  758.6 136.1 %all-gather.15.cloned.1.call-start = ((), (), s32[]{:S(2)}) async-start(), calls=%async_computation.21 | async-start | bytes 4718592 | tf_op jit(solution)/shard_map/all_gather | solution.py:121
  905.2 52.6 %all-to-all-start.4 = ((f32[1024,8,64]{0,2,1:T(8,128)}), f32[1024,8,64]{0,2,1:T(8,128)S(1)}, u32[]{:S(2)}, u32[]{:S(2)}) async-start(f32[1024,8,64]{0,2,1:T(8,128)} %bitcast.142), calls=%async_computation.6 | async-start | bytes 4194304 | tf_op jit(solution)/shard_map/all_to_all | solution.py:59
  908.9 191.9 %reduce-scatter.10.cloned.1.call-start = ((), (), s32[]{:S(2)}) async-start(), calls=%async_computation.22 | async-start | bytes 4718592 | tf_op jit(solution)/shard_map/reduce_scatter | solution.py:116
  958.2 24.7 %collective-permute-start.2 = (f32[4096,64]{0,1:T(8,128)S(1)}, f32[4096,64]{0,1:T(8,128)S(1)}, u32[]{:S(2)}, u32[]{:S(2)}) collective-permute-start(f32[4096,64]{0,1:T(8,128)S(1)} %bitcast.147), channel_id=1, source_target_pairs={{0,2},{1,3},{2,0},{3,1},{4,6},{5,7},{6,4},{7,5},{8,10},{9,11},{10,... | collective-permute-start | bytes 3145736 | tf_op jit(solution)/shard_map/ppermute | solution.py:11
  959.7 25.5 %slice-start.1 = ((f32[14336,64]{1,0:T(8,128)}), f32[2048,64]{1,0:T(8,128)S(1)}, s32[]{:S(2)}) async-start(f32[14336,64]{1,0:T(8,128)} %scatter_custom_fusion), calls=%async_computation.29 | async-start | bytes 2097152 | tf_op jit(solution)/shard_map/slice | solution.py:109
  983.0 12.7 collective-permute-start.3
  996.9 6.4 collective-permute-start.4
  1003.4 10.6 collective-permute-start.5
  1051.8 78.5 %all-gather.17.cloned.1.call-start = ((), (), s32[]{:S(2)}) async-start(), calls=%async_computation.23 | async-start | bytes 2359296 | tf_op jit(solution)/shard_map/all_gather | solution.py:140
  1102.6 270.8 %reduce-scatter.12.cloned.1.call-start = ((), (), s32[]{:S(2)}) async-start(), calls=%async_computation.24 | async-start | bytes 9437184 | tf_op jit(solution)/shard_map/reduce_scatter | solution.py:136
  1187.8 24.6 %collective-permute-start.6 = (f32[4096,64]{0,1:T(8,128)S(1)}, f32[4096,64]{0,1:T(8,128)S(1)}, u32[]{:S(2)}, u32[]{:S(2)}) collective-permute-start(f32[4096,64]{0,1:T(8,128)S(1)} %bitcast.148), channel_id=1, source_target_pairs={{0,2},{1,3},{2,0},{3,1},{4,6},{5,7},{6,4},{7,5},{8,10},{9,11},{10,... | collective-permute-start | bytes 3145736 | tf_op jit(solution)/shard_map/ppermute | solution.py:11
  1212.6 12.5 collective-permute-start.7
  1226.0 6.4 collective-permute-start.8
  1232.5 10.5 collective-permute-start.9
  1284.8 88.6 %copy-start.1 = (f32[4096,64]{0,1:T(8,128)S(1)}, f32[4096,64]{0,1:T(8,128)}, u32[]{:S(2)}) copy-start(f32[4096,64]{0,1:T(8,128)} %reduce-scatter.8.cloned.1.call-done) | copy-start | bytes 3145732
  1284.9 136.2 %all-gather.19.cloned.1.call-start = ((), (), s32[]{:S(2)}) async-start(), calls=%async_computation.25 | async-start | bytes 4718592 | tf_op jit(solution)/shard_map/all_gather | solution.py:140
  1375.6 356.1 %reduce-scatter.14.cloned.1.call-start = ((), (), s32[]{:S(2)}) async-start(), calls=%async_computation.26 | async-start | bytes 18874368 | tf_op jit(solution)/shard_map/reduce_scatter | solution.py:136
  1481.1 24.6 %collective-permute-start.10 = (f32[4096,64]{0,1:T(8,128)S(1)}, f32[4096,64]{0,1:T(8,128)S(1)}, u32[]{:S(2)}, u32[]{:S(2)}) collective-permute-start(f32[4096,64]{0,1:T(8,128)S(1)} %bitcast.149), channel_id=1, source_target_pairs={{0,1},{1,0},{2,3},{3,2},{4,5},{5,4},{6,7},{7,6},{8,9},{9,8},{10,11... | collective-permute-start | bytes 3145736 | tf_op jit(solution)/shard_map/ppermute | solution.py:11
  1505.9 12.5 collective-permute-start.11
  1564.5 167.2 %copy-start = (f32[8192,64]{0,1:T(8,128)S(1)}, f32[8192,64]{0,1:T(8,128)}, u32[]{:S(2)}) copy-start(f32[8192,64]{0,1:T(8,128)} %reduce-scatter.6.cloned.1.call-done) | copy-start | bytes 6291460
  1564.5 250.6 %all-gather.21.cloned.1.call-start = ((), (), s32[]{:S(2)}) async-start(), calls=%async_computation.27 | async-start | bytes 9437184 | tf_op jit(solution)/shard_map/all_gather | solution.py:140
  1880.9 1.0 copy-start.2
Sparse Core Ops, SparseCore 0:
  8.9 42.0 all-gather.10
  52.6 45.5 all-gather.8
  358.2 167.0 reduce-scatter.5
  528.1 80.4 all-gather.12
  758.7 88.3 reduce-scatter.7
  849.4 45.3 all-gather.14
  1051.9 48.7 reduce-scatter.9
  1102.7 27.6 all-gather.16
  1285.0 88.3 reduce-scatter.11
  1375.7 45.3 all-gather.18
  1564.6 167.0 reduce-scatter.13
  1734.6 80.4 all-gather.20
where the time goes:
time: 1900 us; the launch traced here: 1890 us
  waiting for transfers between devices  1100 us (58%)
  blocking collectives  426 us (22%)
  other arithmetic  162 us (9%)
  matrix products  122 us (6%)
  local copies, waits for them, and re-layouts  35 us (2%)
  starting transfers between devices  32.6 us (2%)
    reduce_scatter x3, waiting for transfers between devices, body(): lax.psum_scatter(partial_value, 'elem', scatter_dimension=1, tiled=True)  304 us
    reduce_scatter x2, waiting for transfers between devices, body(): lax.psum_scatter(correction, 'elem', scatter_dimension=1, tiled=True)  256 us
    ppermute x12, waiting for transfers between devices, swapped(): lax.ppermute(array, axis, [(i, i ^ 1 << bit) for i in range(lax.axis_size...  161 us
    all_to_all x3, blocking collectives, from_row_block(): lax.all_to_all(partial_value, 'elem', split_axis=1, concat_axis=0, tiled=...  155 us
    all_gather x3, waiting for transfers between devices, body(): wide_back = lax.all_gather(back_in, 'elem', axis=1, tiled=True)  154 us
    all_to_all x5, blocking collectives, to_row_block(): lax.all_to_all(whole_front, 'elem', split_axis=0, concat_axis=1, tiled=True)  152 us
    scatter-add x1, other arithmetic, form_loads(): term_rows.at[places.T.reshape(-1)]  134 us
    all_gather x2, waiting for transfers between devices, body(): lax.all_gather(solved.astype(jnp.bfloat16), 'elem', axis=1, tiled=True)  126 us
  transfers between devices with their start and end apart: 27, of which 24 were waited for; matrix products, arithmetic and copies ran while one was open for 1% of the time, Pallas kernels for 0%

commit v1 on v0

--- a/solution.py
+++ b/solution.py
@@ -137,7 +137,14 @@
                 correction, "elem", scatter_dimension=1, tiled=True
             )
         back_in = (live_rows * residual).astype(jnp.bfloat16)
-        wide_back = lax.all_gather(back_in, "elem", axis=1, tiled=True)
+        ring = [back_in]
+        for hop in range(7):
+            ring.append(lax.ppermute(ring[-1], "elem", [(dev, (dev + 1) % 8) for dev in range(8)]))
+        wide_back = jnp.roll(
+            jnp.concatenate(ring[::-1], axis=1),
+            (lax.axis_index("elem") + 1) * ring[0].shape[1],
+            axis=1,
+        )
         factor_rows = inverse_factor[offset : offset + block_rows]
         partial_value = lax.dot_general(
             factor_rows, wide_back, (((0,), (0,)), ((), ())), preferred_element_type=jnp.float32

time: 1900 us -> 2000 us (1.053)
  waiting for transfers between devices: 1100 us -> 1180 us
    ppermute x0 -> x21, waiting for transfers between devices: none -> 238 us  [body(): lax.ppermute(ring[-1], 'elem', [(dev, (dev + 1) % 8) for dev in range(8)])]
    all_gather x3 -> x0, waiting for transfers between devices: 154 us -> none  [body(): wide_back = lax.all_gather(back_in, 'elem', axis=1, tiled=True)]
  transfers between devices with their start and end apart: 27 -> 45, of which waited for: 24 -> 42; matrix products, arithmetic and copies ran while one was open for 1% -> 1% of each run, Pallas kernels for 0% -> 0%
where the time goes in v1:
time: 2000 us; the launch traced here: 1990 us
  waiting for transfers between devices  1180 us (59%)
  blocking collectives  426 us (21%)
  other arithmetic  162 us (8%)
  matrix products  120 us (6%)
  local copies, waits for them, and re-layouts  52.5 us (3%)
  starting transfers between devices  33.6 us (2%)
    reduce_scatter x3, waiting for transfers between devices, body(): lax.psum_scatter(partial_value, 'elem', scatter_dimension=1, tiled=True)  304 us
    reduce_scatter x2, waiting for transfers between devices, body(): lax.psum_scatter(correction, 'elem', scatter_dimension=1, tiled=True)  256 us
    ppermute x21, waiting for transfers between devices, body(): lax.ppermute(ring[-1], 'elem', [(dev, (dev + 1) % 8) for dev in range(8)])  238 us
    ppermute x12, waiting for transfers between devices, swapped(): lax.ppermute(array, axis, [(i, i ^ 1 << bit) for i in range(lax.axis_size...  161 us
    all_to_all x3, blocking collectives, from_row_block(): lax.all_to_all(partial_value, 'elem', split_axis=1, concat_axis=0, tiled=...  155 us
    all_to_all x5, blocking collectives, to_row_block(): lax.all_to_all(whole_front, 'elem', split_axis=0, concat_axis=1, tiled=True)  151 us
    scatter-add x1, other arithmetic, form_loads(): term_rows.at[places.T.reshape(-1)]  134 us
    all_gather x2, waiting for transfers between devices, body(): lax.all_gather(solved.astype(jnp.bfloat16), 'elem', axis=1, tiled=True)  126 us
  transfers between devices with their start and end apart: 45, of which 42 were waited for; matrix products, arithmetic and copies ran while one was open for 1% of the time, Pallas kernels for 0%

profile of v1, /device:TPU:0, one launch (start us, length us, event | category | flops | bytes accessed | tf_op | source)
XLA Modules:
  0.0 1992.2 jit_solution(9682564635656947044)
XLA Ops:
  12.6 6.4 all-to-all-start
  19.8 95.4 %all_gather.21 = s32[24,1024]{1,0:T(8,128)S(1)} all-gather(s32[24,128]{1,0:T(8,128)S(1)} %copy-done.4), channel_id=1, replica_groups=mesh['elem'=8,'front'=4] {'elem'}, dimensions={1}, use_global_device_ids=true | all-gather | bytes 110592 | tf_op jit(solution)/shard_map/all_gather | solution.py:86
  118.4 11.1 all-gather
  129.5 12.7 all_gather.24
  148.5 7.4 copy.39
  161.8 9.4 multiply_add_fusion
  171.2 134.3 %scatter_custom_fusion = f32[14336,64]{1,0:T(8,128)} fusion(s32[24576]{0:T(1024)S(1)} %bitcast.152, f32[24576,64]{1,0:T(8,128)} %bitcast.117, f32[]{:T(128)} %constant.69.clone.1), kind=kCustom, calls=%fused_computation.29 | custom fusion | flops 1572864 | bytes 3670528 | tf_op jit(solution)/shard_map/scatter-add | solution.py:22
  313.0 29.2 %all_to_all.184 = bf16[8,1024,64]{1,2,0:T(8,128)(2,1)S(1)} all-to-all(bf16[8,1024,64]{1,2,0:T(8,128)(2,1)S(1)} %bitcast.133), channel_id=1, replica_groups=mesh['elem'=8,'front'=4] {'elem'}, dimensions={0} | all-to-all | bytes 2097152 | tf_op jit(solution)/shard_map/all_to_all | solution.py:55
  342.2 15.8 fusion.8
  358.1 167.1 %reduce-scatter.6.cloned.1.call-done = f32[8192,64]{0,1:T(8,128)} async-done(((f32[8192,512]{0,1:T(8,128)}), f32[8192,64]{0,1:T(8,128)}) %reduce-scatter.6.cloned.1.call-update) | async-done | bytes 2097168 | tf_op jit(solution)/shard_map/reduce_scatter | solution.py:116
  527.9 80.7 %all-gather.10.cloned.1.call-done = bf16[8192,512]{0,1:T(8,128)(2,1)} async-done(((bf16[8192,64]{0,1:T(8,128)(2,1)}), bf16[8192,512]{0,1:T(8,128)(2,1)}) %all-gather.10.cloned.1.call-update) | async-done | bytes 8388624 | tf_op jit(solution)/shard_map/all_gather | solution.py:121
  608.5 15.8 fusion.2
  628.9 49.0 %all-to-all-done.2 = f32[1024,8,64]{0,2,1:T(8,128)} async-done(((f32[1024,8,64]{0,2,1:T(8,128)}), f32[1024,8,64]{0,2,1:T(8,128)}, u32[]{:S(2)}, u32[]{:S(2)}) %all-to-all-start.2) | async-done | bytes 2097184 | tf_op jit(solution)/shard_map/all_to_all | solution.py:59
  685.7 20.9 %collective-permute-done = f32[4096,64]{0,1:T(8,128)} collective-permute-done((f32[4096,64]{0,1:T(8,128)}, f32[4096,64]{0,1:T(8,128)}, u32[]{:S(2)}, u32[]{:S(2)}) %collective-permute-start) | collective-permute-done | bytes 1048608 | tf_op jit(solution)/shard_map/ppermute | solution.py:11
  709.6 11.0 collective-permute-done.1
  721.0 29.9 %all_to_all.185 = bf16[8,1024,64]{1,2,0:T(8,128)(2,1)S(1)} all-to-all(bf16[8,1024,64]{1,2,0:T(8,128)(2,1)S(1)} %bitcast.134), channel_id=1, replica_groups=mesh['elem'=8,'front'=4] {'elem'}, dimensions={0} | all-to-all | bytes 2097152 | tf_op jit(solution)/shard_map/all_to_all | solution.py:55
  750.9 10.1 fusion.23
  761.3 88.3 %reduce-scatter.8.cloned.1.call-done = f32[4096,64]{0,1:T(8,128)} async-done(((f32[4096,512]{0,1:T(8,128)}), f32[4096,64]{0,1:T(8,128)}) %reduce-scatter.8.cloned.1.call-update) | async-done | bytes 1048592 | tf_op jit(solution)/shard_map/reduce_scatter | solution.py:116
  851.7 45.5 %all-gather.12.cloned.1.call-done = bf16[4096,512]{0,1:T(8,128)(2,1)} async-done(((bf16[4096,64]{0,1:T(8,128)(2,1)}), bf16[4096,512]{0,1:T(8,128)(2,1)}) %all-gather.12.cloned.1.call-update) | async-done | bytes 4194320 | tf_op jit(solution)/shard_map/all_gather | solution.py:121
  897.2 10.5 fusion.17
  911.4 48.9 %all-to-all-done.4 = f32[1024,8,64]{0,2,1:T(8,128)S(1)} async-done(((f32[1024,8,64]{0,2,1:T(8,128)}), f32[1024,8,64]{0,2,1:T(8,128)S(1)}, u32[]{:S(2)}, u32[]{:S(2)}) %all-to-all-start.4) | async-done | bytes 2097184 | tf_op jit(solution)/shard_map/all_to_all | solution.py:59
  962.3 23.0 %collective-permute-done.2 = f32[4096,64]{0,1:T(8,128)S(1)} collective-permute-done((f32[4096,64]{0,1:T(8,128)S(1)}, f32[4096,64]{0,1:T(8,128)S(1)}, u32[]{:S(2)}, u32[]{:S(2)}) %collective-permute-start.2) | collective-permute-done | bytes 1048608 | tf_op jit(solution)/shard_map/ppermute | solution.py:11
  988.0 10.1 collective-permute-done.3
  1007.4 9.0 collective-permute-done.5
  1016.8 30.9 %all_to_all.186 = bf16[8,1024,64]{1,2,0:T(8,128)(2,1)S(1)} all-to-all(bf16[8,1024,64]{1,2,0:T(8,128)(2,1)S(1)} %bitcast.135), channel_id=1, replica_groups=mesh['elem'=8,'front'=4] {'elem'}, dimensions={0} | all-to-all | bytes 2097152 | tf_op jit(solution)/shard_map/all_to_all | solution.py:55
  1047.7 6.6 fusion.36
  1054.4 48.9 %reduce-scatter.10.cloned.1.call-done = f32[2048,64]{0,1:T(8,128)} async-done(((f32[2048,512]{0,1:T(8,128)}), f32[2048,64]{0,1:T(8,128)}) %reduce-scatter.10.cloned.1.call-update) | async-done | bytes 524304 | tf_op jit(solution)/shard_map/reduce_scatter | solution.py:116
  1104.5 7.6 collective-permute-done.6
  1112.1 7.6 collective-permute-done.7
  1119.7 7.6 collective-permute-done.8
  1127.3 7.6 collective-permute-done.9
  1134.9 7.6 collective-permute-done.10
  1142.4 7.6 collective-permute-done.11
  1150.0 7.6 collective-permute-done.12
  1163.7 51.9 %all_to_all.187 = f32[1024,8,64]{0,2,1:T(8,128)S(1)} all-to-all(f32[1024,8,64]{0,2,1:T(8,128)S(1)} %bitcast.141), channel_id=1, replica_groups=mesh['elem'=8,'front'=4] {'elem'}, dimensions={1} | all-to-all | bytes 4194304 | tf_op jit(solution)/shard_map/all_to_all | solution.py:59
  1217.7 22.9 %collective-permute-done.13 = f32[4096,64]{0,1:T(8,128)S(1)} collective-permute-done((f32[4096,64]{0,1:T(8,128)S(1)}, f32[4096,64]{0,1:T(8,128)S(1)}, u32[]{:S(2)}, u32[]{:S(2)}) %collective-permute-start.13) | collective-permute-done | bytes 1048608 | tf_op jit(solution)/shard_map/ppermute | solution.py:11
  1242.3 11.0 collective-permute-done.14
  1262.2 9.0 collective-permute-done.16
  1271.5 31.2 %all_to_all.188 = bf16[8,1024,64]{1,2,0:T(8,128)(2,1)S(1)} all-to-all(bf16[8,1024,64]{1,2,0:T(8,128)(2,1)S(1)} %bitcast.136), channel_id=1, replica_groups=mesh['elem'=8,'front'=4] {'elem'}, dimensions={0} | all-to-all | bytes 2097152 | tf_op jit(solution)/shard_map/all_to_all | solution.py:55
  1302.7 10.1 fusion.26
  1312.9 88.5 %reduce-scatter.12.cloned.1.call-done = f32[4096,64]{0,1:T(8,128)} async-done(((f32[4096,512]{0,1:T(8,128)}), f32[4096,64]{0,1:T(8,128)}) %reduce-scatter.12.cloned.1.call-update) | async-done | bytes 1048592 | tf_op jit(solution)/shard_map/reduce_scatter | solution.py:136
  1402.8 10.4 collective-permute-done.17
  1413.2 10.4 collective-permute-done.18
  1423.6 10.4 collective-permute-done.19
  1434.0 10.4 collective-permute-done.20
  1444.4 10.4 collective-permute-done.21
  1454.8 10.4 collective-permute-done.22
  1465.2 10.4 collective-permute-done.23
  1476.3 6.9 fusion.19
  1483.3 51.5 %all_to_all.189 = f32[1024,8,64]{0,2,1:T(8,128)S(1)} all-to-all(f32[1024,8,64]{0,2,1:T(8,128)S(1)} %bitcast.142), channel_id=1, replica_groups=mesh['elem'=8,'front'=4] {'elem'}, dimensions={1} | all-to-all | bytes 4194304 | tf_op jit(solution)/shard_map/all_to_all | solution.py:59
  1536.7 23.0 %collective-permute-done.24 = f32[4096,64]{0,1:T(8,128)S(1)} collective-permute-done((f32[4096,64]{0,1:T(8,128)S(1)}, f32[4096,64]{0,1:T(8,128)S(1)}, u32[]{:S(2)}, u32[]{:S(2)}) %collective-permute-start.24) | collective-permute-done | bytes 1048608 | tf_op jit(solution)/shard_map/ppermute | solution.py:11
  1561.4 11.0 collective-permute-done.25
  1572.7 30.1 %all_to_all.190 = bf16[8,1024,64]{1,2,0:T(8,128)(2,1)S(1)} all-to-all(bf16[8,1024,64]{1,2,0:T(8,128)(2,1)S(1)} %bitcast.137), channel_id=1, replica_groups=mesh['elem'=8,'front'=4] {'elem'}, dimensions={0} | all-to-all | bytes 2097152 | tf_op jit(solution)/shard_map/all_to_all | solution.py:55
  1602.8 15.7 fusion.11
  1618.5 167.2 %reduce-scatter.14.cloned.1.call-done = f32[8192,64]{0,1:T(8,128)} async-done(((f32[8192,512]{0,1:T(8,128)}), f32[8192,64]{0,1:T(8,128)}) %reduce-scatter.14.cloned.1.call-update) | async-done | bytes 2097168 | tf_op jit(solution)/shard_map/reduce_scatter | solution.py:136
  1787.6 16.0 collective-permute-done.26
  1803.6 16.0 collective-permute-done.27
  1819.6 16.0 collective-permute-done.28
  1835.7 16.0 collective-permute-done.29
  1851.7 16.0 collective-permute-done.30
  1867.7 16.0 collective-permute-done.31
  1883.9 16.0 collective-permute-done.32
  1917.0 14.3 fusion.4
  1931.3 51.6 %all_to_all.191 = f32[1024,8,64]{0,2,1:T(8,128)S(1)} all-to-all(f32[1024,8,64]{0,2,1:T(8,128)S(1)} %bitcast.140), channel_id=1, replica_groups=mesh['elem'=8,'front'=4] {'elem'}, dimensions={1} | all-to-all | bytes 4194304 | tf_op jit(solution)/shard_map/all_to_all | solution.py:59
  (186 shorter events, 116.2 us)
Async XLA Ops:
  6.5 13.2 copy-start.4
  6.5 111.2 %copy-start.6 = (s32[7]{0:T(128)S(1)}, s32[7]{0:T(128)}, u32[]{:S(2)}) copy-start(s32[7]{0:T(128)} %param.17) | copy-start | bytes 88
  6.5 111.9 %copy-start.7 = (s32[128]{0:T(128)S(1)}, s32[128]{0:T(128)}, u32[]{:S(2)}) copy-start(s32[128]{0:T(128)} %param.13) | copy-start | bytes 1540
  6.5 123.0 %copy-start.5 = (bf16[24,128]{1,0:T(8,128)(2,1)S(1)}, bf16[24,128]{1,0:T(8,128)(2,1)}, u32[]{:S(2)}) copy-start(bf16[24,128]{1,0:T(8,128)(2,1)} %param.11) | copy-start | bytes 18436
  6.5 137.4 %all-gather.8.cloned.1.call-start = ((), (), s32[]{:S(2)}) async-start(), calls=%async_computation.17 | async-start | bytes 1327104 | tf_op jit(solution)/shard_map/all_gather | solution.py:81
  12.6 143.3 %all-to-all-start = ((bf16[128,24,512]{0,1,2:T(8,128)(2,1)}), bf16[128,24,512]{0,1,2:T(8,128)(2,1)S(1)}, u32[]{:S(2)}, u32[]{:S(2)}) async-start(bf16[128,24,512]{0,1,2:T(8,128)(2,1)} %copy.36), calls=%async_computation | async-start | bytes 6291456 | tf_op jit(solution)/shard_map/all_to_all | solution.py:78
  19.0 129.5 %all-gather.6.cloned.1.call-start = ((), (), s32[]{:S(2)}) async-start(), calls=%async_computation.16 | async-start | bytes 1327104 | tf_op jit(solution)/shard_map/all_gather | solution.py:80
  19.7 505.4 %reduce-scatter.6.cloned.1.call-start = ((), (), s32[]{:S(2)}) async-start(), calls=%async_computation.18 | async-start | bytes 18874368 | tf_op jit(solution)/shard_map/reduce_scatter | solution.py:116
  358.0 250.5 %all-gather.10.cloned.1.call-start = ((), (), s32[]{:S(2)}) async-start(), calls=%async_computation.19 | async-start | bytes 9437184 | tf_op jit(solution)/shard_map/all_gather | solution.py:121
  624.3 59.5 %slice-start = ((f32[14336,64]{1,0:T(8,128)}), f32[4096,64]{1,0:T(8,128)S(1)}, s32[]{:S(2)}) async-start(f32[14336,64]{1,0:T(8,128)} %scatter_custom_fusion), calls=%async_computation.25 | async-start | bytes 4194304 | tf_op jit(solution)/shard_map/slice | solution.py:109
  624.3 53.5 %all-to-all-start.2 = ((f32[1024,8,64]{0,2,1:T(8,128)}), f32[1024,8,64]{0,2,1:T(8,128)}, u32[]{:S(2)}, u32[]{:S(2)}) async-start(f32[1024,8,64]{0,2,1:T(8,128)} %bitcast.138), calls=%async_computation.3 | async-start | bytes 4194304 | tf_op jit(solution)/shard_map/all_to_all | solution.py:59
  628.8 220.8 %reduce-scatter.8.cloned.1.call-start = ((), (), s32[]{:S(2)}) async-start(), calls=%async_computation.20 | async-start | bytes 9437184 | tf_op jit(solution)/shard_map/reduce_scatter | solution.py:116
  681.7 24.9 %collective-permute-start = (f32[4096,64]{0,1:T(8,128)}, f32[4096,64]{0,1:T(8,128)}, u32[]{:S(2)}, u32[]{:S(2)}) collective-permute-start(f32[4096,64]{0,1:T(8,128)} %bitcast.67), channel_id=1, source_target_pairs={{0,1},{1,0},{2,3},{3,2},{4,5},{5,4},{6,7},{7,6},{8,9},{9,8},{10,11... | collective-permute-start | bytes 3145736 | tf_op jit(solution)/shard_map/ppermute | solution.py:11
  708.1 12.6 collective-permute-start.1
  761.1 136.1 %all-gather.12.cloned.1.call-start = ((), (), s32[]{:S(2)}) async-start(), calls=%async_computation.21 | async-start | bytes 4718592 | tf_op jit(solution)/shard_map/all_gather | solution.py:121
  907.7 52.6 %all-to-all-start.4 = ((f32[1024,8,64]{0,2,1:T(8,128)}), f32[1024,8,64]{0,2,1:T(8,128)S(1)}, u32[]{:S(2)}, u32[]{:S(2)}) async-start(f32[1024,8,64]{0,2,1:T(8,128)} %bitcast.139), calls=%async_computation.6 | async-start | bytes 4194304 | tf_op jit(solution)/shard_map/all_to_all | solution.py:59
  911.3 76.4 %slice-start.1 = ((f32[14336,64]{1,0:T(8,128)}), f32[2048,64]{1,0:T(8,128)S(1)}, s32[]{:S(2)}) async-start(f32[14336,64]{1,0:T(8,128)} %scatter_custom_fusion), calls=%async_computation.26 | async-start | bytes 2097152 | tf_op jit(solution)/shard_map/slice | solution.py:109
  911.3 191.9 %reduce-scatter.10.cloned.1.call-start = ((), (), s32[]{:S(2)}) async-start(), calls=%async_computation.22 | async-start | bytes 4718592 | tf_op jit(solution)/shard_map/reduce_scatter | solution.py:116
  960.6 24.7 %collective-permute-start.2 = (f32[4096,64]{0,1:T(8,128)S(1)}, f32[4096,64]{0,1:T(8,128)S(1)}, u32[]{:S(2)}, u32[]{:S(2)}) collective-permute-start(f32[4096,64]{0,1:T(8,128)S(1)} %bitcast.143), channel_id=1, source_target_pairs={{0,2},{1,3},{2,0},{3,1},{4,6},{5,7},{6,4},{7,5},{8,10},{9,11},{10,... | collective-permute-start | bytes 3145736 | tf_op jit(solution)/shard_map/ppermute | solution.py:11
  985.5 12.7 collective-permute-start.3
  999.3 6.4 collective-permute-start.4
  1005.9 10.6 collective-permute-start.5
  1054.3 347.1 %reduce-scatter.12.cloned.1.call-start = ((), (), s32[]{:S(2)}) async-start(), calls=%async_computation.23 | async-start | bytes 9437184 | tf_op jit(solution)/shard_map/reduce_scatter | solution.py:136
  1103.2 55.9 %copy-start.1 = (f32[2048,64]{0,1:T(8,128)S(1)}, f32[2048,64]{0,1:T(8,128)}, u32[]{:S(2)}) copy-start(f32[2048,64]{0,1:T(8,128)} %reduce-scatter.10.cloned.1.call-done) | copy-start | bytes 1572868
  1104.4 7.6 collective-permute-start.6
  1112.1 7.6 collective-permute-start.7
  1119.7 7.6 collective-permute-start.8
  1127.3 7.6 collective-permute-start.9
  1134.8 7.6 collective-permute-start.10
  1142.4 7.6 collective-permute-start.11
  1150.0 7.6 collective-permute-start.12
  1216.0 24.6 %collective-permute-start.13 = (f32[4096,64]{0,1:T(8,128)S(1)}, f32[4096,64]{0,1:T(8,128)S(1)}, u32[]{:S(2)}, u32[]{:S(2)}) collective-permute-start(f32[4096,64]{0,1:T(8,128)S(1)} %bitcast.144), channel_id=1, source_target_pairs={{0,2},{1,3},{2,0},{3,1},{4,6},{5,7},{6,4},{7,5},{8,10},{9,11},{10,... | collective-permute-start | bytes 3145736 | tf_op jit(solution)/shard_map/ppermute | solution.py:11
  1240.8 12.5 collective-permute-start.14
  1254.2 6.4 collective-permute-start.15
  1260.7 10.5 collective-permute-start.16
  1312.8 88.6 %copy-start.2 = (f32[4096,64]{0,1:T(8,128)S(1)}, f32[4096,64]{0,1:T(8,128)}, u32[]{:S(2)}) copy-start(f32[4096,64]{0,1:T(8,128)} %reduce-scatter.8.cloned.1.call-done) | copy-start | bytes 3145732
  1312.8 472.9 %reduce-scatter.14.cloned.1.call-start = ((), (), s32[]{:S(2)}) async-start(), calls=%async_computation.24 | async-start | bytes 18874368 | tf_op jit(solution)/shard_map/reduce_scatter | solution.py:136
  1402.8 10.5 collective-permute-start.17
  1413.2 10.4 collective-permute-start.18
  1423.6 10.4 collective-permute-start.19
  1434.0 10.4 collective-permute-start.20
  1444.4 10.4 collective-permute-start.21
  1454.8 10.4 collective-permute-start.22
  1465.2 10.4 collective-permute-start.23
  1535.1 24.6 %collective-permute-start.24 = (f32[4096,64]{0,1:T(8,128)S(1)}, f32[4096,64]{0,1:T(8,128)S(1)}, u32[]{:S(2)}, u32[]{:S(2)}) collective-permute-start(f32[4096,64]{0,1:T(8,128)S(1)} %bitcast.145), channel_id=1, source_target_pairs={{0,1},{1,0},{2,3},{3,2},{4,5},{5,4},{6,7},{7,6},{8,9},{9,8},{10,11... | collective-permute-start | bytes 3145736 | tf_op jit(solution)/shard_map/ppermute | solution.py:11
  1559.9 12.5 collective-permute-start.25
  1618.5 167.2 %copy-start = (f32[8192,64]{0,1:T(8,128)S(1)}, f32[8192,64]{0,1:T(8,128)}, u32[]{:S(2)}) copy-start(f32[8192,64]{0,1:T(8,128)} %reduce-scatter.6.cloned.1.call-done) | copy-start | bytes 6291460
  1787.5 16.1 collective-permute-start.26
  1803.6 16.0 collective-permute-start.27
  1819.6 16.0 collective-permute-start.28
  1835.7 16.0 collective-permute-start.29
  1851.7 16.0 collective-permute-start.30
  1867.7 16.0 collective-permute-start.31
  1883.7 16.2 collective-permute-start.32
  1931.3 52.0 %copy-start.3 = (f32[2048,64]{0,1:T(8,128)S(1)}, f32[2048,64]{0,1:T(8,128)}, u32[]{:S(2)}) copy-start(f32[2048,64]{0,1:T(8,128)} %get-tuple-element.8) | copy-start | bytes 1572868
Sparse Core Ops, SparseCore 0:
  8.9 42.0 all-gather.7
  52.6 45.4 all-gather.5
  358.1 166.9 reduce-scatter.5
  528.0 80.4 all-gather.9
  761.2 88.3 reduce-scatter.7
  851.9 45.3 all-gather.11
  1054.4 48.7 reduce-scatter.9
  1313.0 88.3 reduce-scatter.11
  1618.6 167.0 reduce-scatter.13
